TPU v7x, 512 devices: a whole 4x4x16 slice. The times are simulated.
512 devices in a mesh: dp: 16 (over x, y), heads: 16 (over z), side: 2 (over core).
Axes of the slice: x: 4, y: 4, z: 16, core: 2. Of those that a mesh axis runs over, the one named last changes fastest.
Arguments:
- queries: bfloat16 [384, 2, 4096], P('dp', None, ('heads', 'side')), may hold values from -6 to 6
- new_keys: bfloat16 [384, 2, 4096], P('dp', None, ('heads', 'side')), may hold values from -6 to 6
- new_values: bfloat16 [384, 2, 4096], P('dp', None, ('heads', 'side')), may hold values from -6 to 6
- head_states: bfloat16 [384, 32, 128, 128], P('dp', ('heads', 'side')), may hold values from -6 to 6
- slopes: float32 [32], P(('heads', 'side')), may hold values from 0.004 to 0.9
- head_gain: float32 [4096], P(('heads', 'side')), may hold values from 0.5 to 1.5
- out_weight: bfloat16 [4096, 3072], P(('heads', 'side')), may hold values from -0.1875 to 0.1875
- residual: bfloat16 [384, 2, 3072], P('dp', None, ('heads', 'side')), may hold values from -10 to 10
- norm_gain: float32 [3072], replicated, may hold values from 0.5 to 1.5
- expert_ids: int32 [384, 2, 2], P('dp'), may hold values from 0 to 15, all different within a row; in each aligned block of 48 rows (0 to 47, 48 to 95, ..., all dimensions but the last counted through in order) at most 9 rows name the same one
- expert_gates: float32 [384, 2, 2], P('dp'), may hold values from 0.2 to 1
- w_gate: bfloat16 [16, 16, 192, 4608], P('dp', None, 'side', 'heads'), may hold values from -0.109375 to 0.109375
- w_up: bfloat16 [16, 16, 192, 4608], P('dp', None, 'side', 'heads'), may hold values from -0.109375 to 0.109375
- w_down: bfloat16 [16, 4608, 16, 192], P('dp', 'heads', None, 'side'), may hold values from -0.125 to 0.125
Outputs:
- state_out: bfloat16 [384, 32, 128, 128], P('dp', ('heads', 'side'))
- resid_out: bfloat16 [384, 2, 3072], P('dp', None, ('heads', 'side'))
- moe_out: bfloat16 [384, 2, 3072], P('dp', None, ('heads', 'side'))
Inputs may be any that keep to these rules, and one draw needn't show every extreme that they name: `expert_ids`: among the 48 tokens of one dp index a token's 2 experts differ, no expert is chosen by more than 9 of them, and some expert is chosen by exactly 9.
All inputs are finite; a program needn't handle non-finite values.
Results may differ from a plain program's by a relative error of at most 0.025.
Values may be sent and summed in bfloat16 or wider, within the bound.
A program may use at most 64 MiB of HBM per device.

v0:
```python
import jax
import jax.numpy as jnp
from jax import lax
from jax.sharding import PartitionSpec as P


def local(
    queries,
    new_keys,
    new_values,
    head_states,
    slopes,
    head_gain,
    out_weight,
    residual,
    norm_gain,
    expert_ids,
    expert_gates,
    w_gate,
    w_up,
    w_down,
):
    requests_dev, step_count, inner_width = queries.shape
    local_heads = slopes.shape[0]
    head_size = inner_width // local_heads
    query_rows = queries.astype(jnp.float32).reshape(
        requests_dev, step_count, local_heads, head_size
    )
    key_rows = new_keys.astype(jnp.float32).reshape(
        requests_dev, step_count, local_heads, head_size
    )
    value_rows = new_values.astype(jnp.float32).reshape(
        requests_dev, step_count, local_heads, head_size
    )
    decays = jnp.exp(-slopes)[None, :, None, None]
    current = head_states.astype(jnp.float32)
    outputs = []
    for step in range(step_count):
        current = decays * current + key_rows[:, step, :, :, None] * value_rows[:, step, :, None, :]
        outputs.append(
            jnp.einsum(
                "rhi,rhij->rhj", query_rows[:, step], current, precision=lax.Precision.HIGHEST
            )
        )
    state_out = current.astype(jnp.bfloat16)
    head_output = jnp.stack(outputs, 1)
    scaled = head_output * lax.rsqrt(jnp.mean(head_output * head_output, -1, keepdims=True) + 1e-06)
    tokens_dev = requests_dev * step_count
    normed = (
        (scaled * head_gain.reshape(local_heads, head_size))
        .astype(jnp.bfloat16)
        .reshape(tokens_dev, inner_width)
    )
    partial_out = jnp.dot(normed, out_weight, preferred_element_type=jnp.float32)
    attention = lax.psum_scatter(partial_out, ("heads", "side"), scatter_dimension=1, tiled=True)
    width = norm_gain.shape[0]
    piece_width = attention.shape[1]
    resid_new = (residual.reshape(tokens_dev, piece_width).astype(jnp.float32) + attention).astype(
        jnp.bfloat16
    )
    stream = resid_new.astype(jnp.float32)
    sum_squares = lax.psum(jnp.sum(stream * stream, 1), ("heads", "side"))
    gain_piece = lax.dynamic_slice_in_dim(
        norm_gain, lax.axis_index(("heads", "side")) * piece_width, piece_width
    )
    mixed_in = (stream * lax.rsqrt(sum_squares / width + 1e-06)[:, None] * gain_piece).astype(
        jnp.bfloat16
    )
    groups = lax.axis_size("dp")
    heads_count = lax.axis_size("heads")
    choices_each = expert_ids.shape[2]
    capacity = max(2, 3 * choices_each * tokens_dev // (2 * groups))
    flat_ids = expert_ids.reshape(-1)
    onehot_table = (flat_ids[:, None] == jnp.arange(groups, dtype=jnp.int32)[None, :]).astype(
        jnp.int32
    )
    earlier = jnp.cumsum(onehot_table, 0) - onehot_table
    slot_index = jnp.sum(earlier * onehot_table, 1)
    target = flat_ids * capacity + slot_index
    source_row = jnp.arange(tokens_dev * choices_each, dtype=jnp.int32) // choices_each
    gate_flat = w_gate[0].reshape(-1, w_gate.shape[3])
    up_flat = w_up[0].reshape(-1, w_up.shape[3])
    down_flat = w_down[0].reshape(w_down.shape[1], -1)
    holder = jnp.zeros((groups * capacity, mixed_in.shape[1]), mixed_in.dtype)
    arrived = lax.all_to_all(
        holder.at[target].set(mixed_in[source_row]).reshape(groups, capacity, mixed_in.shape[1]),
        "dp",
        split_axis=0,
        concat_axis=0,
        tiled=True,
    )
    piece = lax.all_gather(arrived, "heads", axis=2, tiled=True)
    flat_piece = piece.reshape(-1, piece.shape[2])
    gate_part = jnp.dot(flat_piece, gate_flat, preferred_element_type=jnp.float32)
    up_part = jnp.dot(flat_piece, up_flat, preferred_element_type=jnp.float32)
    gate_val, up_val = (
        lax.psum(gate_part.astype(jnp.bfloat16), "side").astype(jnp.float32),
        lax.psum(up_part.astype(jnp.bfloat16), "side").astype(jnp.float32),
    )
    activation = (jax.nn.silu(gate_val) * up_val).astype(jnp.bfloat16)
    down_part = jnp.dot(activation, down_flat, preferred_element_type=jnp.float32).reshape(
        groups, capacity, heads_count, piece_width
    )
    reduced = lax.psum_scatter(
        down_part.astype(jnp.bfloat16), "heads", scatter_dimension=2, tiled=True
    )
    returned = lax.all_to_all(reduced, "dp", split_axis=0, concat_axis=0, tiled=True)
    picked = returned.reshape(groups * capacity, piece_width)[target].astype(jnp.float32)
    weighted = picked * expert_gates.reshape(-1)[:, None]
    moe_out = jnp.sum(weighted.reshape(tokens_dev, choices_each, piece_width), 1).astype(
        jnp.bfloat16
    )
    return (
        state_out,
        resid_new.reshape(requests_dev, step_count, piece_width),
        moe_out.reshape(requests_dev, step_count, piece_width),
    )


def solution(mesh):
    return jax.shard_map(
        local,
        mesh=mesh,
        in_specs=(
            P("dp", None, ("heads", "side")),
            P("dp", None, ("heads", "side")),
            P("dp", None, ("heads", "side")),
            P("dp", ("heads", "side"), None, None),
            P(("heads", "side")),
            P(("heads", "side")),
            P(("heads", "side"), None),
            P("dp", None, ("heads", "side")),
            P(),
            P("dp", None, None),
            P("dp", None, None),
            P("dp", None, "side", "heads"),
            P("dp", None, "side", "heads"),
            P("dp", "heads", None, "side"),
        ),
        out_specs=(
            P("dp", ("heads", "side"), None, None),
            P("dp", None, ("heads", "side")),
            P("dp", None, ("heads", "side")),
        ),
        check_vma=False,
    )
```

profile of v0, /device:TPU:32, one launch (start us, length us, event | category | flops | bytes accessed | tf_op | source)
XLA Modules:
  0.0 491.2 jit_solution(13953203980056573112)
XLA Ops:
  7.2 0.8 bitcast_convert_fusion.1
  8.1 0.7 bitcast_convert_fusion
  9.6 0.7 copy.73
  10.3 2.2 fusion.5
  12.5 1.8 fusion.8
  14.6 1.6 convolution_bitcast_fusion
  17.0 0.8 dynamic_slice.3
  17.9 110.4 %reduce-scatter.7.cloned.1.call-done = f32[96,48]{1,0:T(8,128)} async-done(((f32[3072,48]{1,0:T(8,128)}), f32[96,48]{1,0:T(8,128)}) %reduce-scatter.7.cloned.1.call-update) | async-done | bytes 18448
  128.3 0.9 copy.61
  129.3 46.0 %psum.21 = f32[48]{0:T(128)S(1)} all-reduce(f32[48]{0:T(128)S(1)} %get-tuple-element.5), channel_id=1, replica_groups=mesh['dp'=16,'heads'=16,'side'=2] {'heads','side'}, use_global_device_ids=true, to_apply=%region_5.6 | all-reduce | flops 48 | bytes 384 | tf_op jit(solution)/shard_map/psum | solution.py:62
  175.4 1.0 scatter_custom_fusion
  176.6 14.1 %all_to_all.10 = bf16[16,2,432]{2,1,0:T(2,128)(2,1)S(1)} all-to-all(bf16[16,2,432]{2,1,0:T(2,128)(2,1)S(1)} %reshape.300), channel_id=1, replica_groups=mesh['dp'=16,'heads'=16,'side'=2] {'dp'}, dimensions={0} | all-to-all | bytes 55296 | tf_op jit(solution)/shard_map/all_to_all | solution.py:85
  190.8 0.4 copy.44
  191.2 83.1 %all_gather.3 = bf16[16,9,1536]{1,0,2:T(8,128)(2,1)} all-gather(bf16[16,9,96]{1,0,2:T(8,128)(2,1)S(1)} %copy.44), channel_id=1, replica_groups=mesh['dp'=16,'heads'=16,'side'=2] {'heads'}, dimensions={2}, use_global_device_ids=true | all-gather | bytes 470016 | tf_op jit(solution)/shard_map/all_gather | solution.py:92
  274.3 8.2 %reshape.288 = bf16[144,1536]{0,1:T(8,128)(2,1)S(1)} reshape(bf16[16,9,1536]{1,0,2:T(8,128)(2,1)} %all_gather.3) | data formatting | bytes 884736 | tf_op jit(solution)/shard_map/reshape | solution.py:93
  282.5 1.1 convolution_convert_fusion.1
  283.6 0.2 copy-done.1
  283.8 1.1 convolution_convert_fusion.2
  285.0 2.4 reshape_squeeze.11
  287.3 0.7 copy.46
  288.1 36.6 %all-reduce.7.cloned.1.call-done = (bf16[144,288]{1,0:T(8,128)(2,1)}, bf16[144,288]{1,0:T(8,128)(2,1)}) async-done(((bf16[144,288]{1,0:T(8,128)(2,1)}, bf16[144,288]{1,0:T(8,128)(2,1)}), (bf16[144,288]{1,0:T(8,128)(2,1)}, bf16[144,288]{1,0:T(8,128)(2,1)})) %all-reduce.7.cloned.1.call-update) | async-done | bytes 165904 | tf_op jit(solution)/shard_map/psum | solution.py:98
  324.7 1.0 fusion.23
  325.8 1.6 convolution_convert_fusion
  327.4 1.3 dynamic-slice
  328.7 1.7 fusion.4
  330.5 136.0 %all-reduce.5.cloned.1.call-done = bf16[16,9,16,96]{3,0,2,1:T(8,128)(2,1)} async-done(((bf16[16,9,16,96]{3,0,2,1:T(8,128)(2,1)}), bf16[16,9,16,96]{3,0,2,1:T(8,128)(2,1)}) %all-reduce.5.cloned.1.call-update) | async-done | bytes 442384
  466.5 1.4 constant_dynamic-slice_fusion
  467.9 0.7 reshape.302
  468.6 6.8 %all-to-all-start.1 = ((bf16[16,2,432]{2,1,0:T(2,128)(2,1)}), bf16[16,2,432]{2,1,0:T(2,128)(2,1)S(1)}, u32[]{:S(2)}, u32[]{:S(2)}) async-start(bf16[16,2,432]{2,1,0:T(2,128)(2,1)} %reshape.302), calls=%async_computation.1 | async-start | bytes 65536 | tf_op jit(solution)/shard_map/all_to_all | solution.py:107
  475.6 7.5 %all-to-all-done.1 = bf16[16,2,432]{2,1,0:T(2,128)(2,1)S(1)} async-done(((bf16[16,2,432]{2,1,0:T(2,128)(2,1)}), bf16[16,2,432]{2,1,0:T(2,128)(2,1)S(1)}, u32[]{:S(2)}, u32[]{:S(2)}) %all-to-all-start.1) | async-done | bytes 27680 | tf_op jit(solution)/shard_map/all_to_all | solution.py:107
  483.2 0.7 gather_fusion
  483.9 0.7 fusion.25
  (54 shorter events, 2.2 us)
Async XLA Ops:
  7.2 275.4 %copy-start = (bf16[1,16,96,288]{3,2,1,0:T(8,128)(2,1)S(1)}, bf16[1,16,96,288]{3,2,1,0:T(8,128)(2,1)}, u32[]{:S(2)}) copy-start(bf16[1,16,96,288]{3,2,1,0:T(8,128)(2,1)} %param.26) | copy-start | bytes 2654212
  7.2 5.3 %copy-start.2 = (bf16[24,1,128,128]{3,2,1,0:T(8,128)(2,1)S(1)}, bf16[24,1,128,128]{3,2,1,0:T(8,128)(2,1)}, u32[]{:S(2)}) copy-start(bf16[24,1,128,128]{3,2,1,0:T(8,128)(2,1)} %param.17) | copy-start | bytes 2359300
  7.2 121.1 %reduce-scatter.7.cloned.1.call-start = ((), (), s32[]{:S(2)}) async-start(), calls=%async_computation.3 | async-start | bytes 1622016
  12.5 2.0 copy-start.4
  12.5 2.1 copy-start.9
  14.5 1.7 copy-start.7
  16.2 113.0 %copy-start.6 = (bf16[24,2,96]{2,1,0:T(2,128)(2,1)S(1)}, bf16[24,2,96]{2,1,0:T(2,128)(2,1)}, u32[]{:S(2)}) copy-start(bf16[24,2,96]{2,1,0:T(2,128)(2,1)} %param.21) | copy-start | bytes 27652
  16.2 308.5 %all-reduce.7.cloned.1.call-start = ((), (), s32[]{:S(2)}) async-start(), calls=%async_computation.5 | async-start | bytes 442368 | tf_op jit(solution)/shard_map/psum | solution.py:98
  129.3 145.0 %copy-start.5 = (bf16[48,96]{1,0:T(8,128)(2,1)}, bf16[48,96]{1,0:T(8,128)(2,1)S(1)}, u32[]{:S(2)}) copy-start(bf16[48,96]{1,0:T(8,128)(2,1)S(1)} %get-tuple-element.6) | copy-start | bytes 27652
  282.5 1.3 copy-start.1
  284.9 181.6 %all-reduce.5.cloned.1.call-start = ((), (), s32[]{:S(2)}) async-start(), calls=%async_computation.4 | async-start | bytes 1179648
  288.0 40.7 %copy-start.3 = (bf16[24,1,128,128]{3,2,1,0:T(8,128)(2,1)S(1)}, bf16[24,1,128,128]{3,2,1,0:T(8,128)(2,1)}, u32[]{:S(2)}) copy-start(bf16[24,1,128,128]{3,2,1,0:T(8,128)(2,1)} %param.17) | copy-start | bytes 2359300
  327.4 148.1 %copy-start.8 = (f32[24,2,2]{0,2,1:T(2,128)S(1)}, f32[24,2,2]{0,2,1:T(2,128)}, u32[]{:S(2)}) copy-start(f32[24,2,2]{0,2,1:T(2,128)} %param.24) | copy-start | bytes 1156
  468.6 14.4 %all-to-all-start.1 = ((bf16[16,2,432]{2,1,0:T(2,128)(2,1)}), bf16[16,2,432]{2,1,0:T(2,128)(2,1)S(1)}, u32[]{:S(2)}, u32[]{:S(2)}) async-start(bf16[16,2,432]{2,1,0:T(2,128)(2,1)} %reshape.302), calls=%async_computation.1 | async-start | bytes 65536 | tf_op jit(solution)/shard_map/all_to_all | solution.py:107
Sparse Core Ops, SparseCore 0:
  16.3 111.9 reduce-scatter.6
  285.0 39.6 all-reduce.6
  327.5 138.9 all-reduce.4
where the time goes:
time: 492 us; the launch traced here: 491 us
  waiting for transfers between devices  291 us (59%)
  blocking collectives  143 us (29%)
  local copies, waits for them, and re-layouts  20.6 us (4%)
  between operations  14.7 us (3%)
  matrix products  9.36 us (2%)
  starting transfers between devices  6.93 us (1%)
  other arithmetic  5.83 us (1%)
    unnamed x5, waiting for transfers between devices  246 us
    all_gather x1, blocking collectives, local(): piece = lax.all_gather(arrived, 'heads', axis=2, tiled=True)  83.1 us
    psum x1, blocking collectives, local(): sum_squares = lax.psum(jnp.sum(stream * stream, 1), ('heads', 'side'))  46 us
    psum x1, waiting for transfers between devices, local(): lax.psum(up_part.astype(jnp.bfloat16), 'side').astype(jnp.float32)  36.6 us
    all_to_all x1, blocking collectives, local(): lax.all_to_all(holder.at[target].set(mixed_in[source_row]).reshape(groups...  14.1 us
  transfers between devices with their start and end apart: 4, of which 4 were waited for; matrix products, arithmetic and copies ran while one was open for 2% of the time, Pallas kernels for 0%

commit v1 on v0

--- a/solution.py
+++ b/solution.py
@@ -2,6 +2,11 @@
 import jax.numpy as jnp
 from jax import lax
 from jax.sharding import PartitionSpec as P
+
+
+def axis_by_axis(value, first, second):
+    half = lax.psum(value, first)
+    return lax.psum(half, second)
 
 
 def local(
@@ -59,7 +64,7 @@
         jnp.bfloat16
     )
     stream = resid_new.astype(jnp.float32)
-    sum_squares = lax.psum(jnp.sum(stream * stream, 1), ("heads", "side"))
+    sum_squares = axis_by_axis(jnp.sum(stream * stream, 1), "side", "heads")
     gain_piece = lax.dynamic_slice_in_dim(
         norm_gain, lax.axis_index(("heads", "side")) * piece_width, piece_width
     )

time: 492 us -> 469 us (0.953)
  blocking collectives: 143 us -> 123 us
    psum x1 -> x2, blocking collectives: 46 us -> 33.2 us  [the longest x1 30.7 us: axis_by_axis(): return lax.psum(half, second)]
    all_gather x1, blocking collectives: 83.1 us -> 75.2 us  [local(): piece = lax.all_gather(arrived, 'heads', axis=2, tiled=True)]
where the time goes in v1:
time: 469 us; the launch traced here: 468 us
  waiting for transfers between devices  288 us (61%)
  blocking collectives  123 us (26%)
  local copies, waits for them, and re-layouts  20.6 us (4%)
  between operations  14.7 us (3%)
  matrix products  9.36 us (2%)
  starting transfers between devices  6.93 us (1%)
  other arithmetic  5.83 us (1%)
    unnamed x5, waiting for transfers between devices  246 us
    all_gather x1, blocking collectives, local(): piece = lax.all_gather(arrived, 'heads', axis=2, tiled=True)  75.2 us
    psum x1, waiting for transfers between devices, local(): lax.psum(up_part.astype(jnp.bfloat16), 'side').astype(jnp.float32)  34.3 us
    psum x1, blocking collectives, axis_by_axis(): return lax.psum(half, second)  30.7 us
    all_to_all x1, blocking collectives, local(): lax.all_to_all(holder.at[target].set(mixed_in[source_row]).reshape(groups...  14.2 us
  transfers between devices with their start and end apart: 4, of which 4 were waited for; matrix products, arithmetic and copies ran while one was open for 2% of the time, Pallas kernels for 0%

profile of v1, /device:TPU:32, one launch (start us, length us, event | category | flops | bytes accessed | tf_op | source)
XLA Modules:
  0.0 468.3 jit_solution(3205356275488727703)
XLA Ops:
  7.2 0.8 bitcast_convert_fusion.1
  8.1 0.7 bitcast_convert_fusion
  9.6 0.7 copy.73
  10.3 2.2 fusion.5
  12.5 1.8 fusion.8
  14.6 1.6 convolution_bitcast_fusion
  17.0 0.8 dynamic_slice.3
  17.9 110.4 %reduce-scatter.7.cloned.1.call-done = f32[96,48]{1,0:T(8,128)} async-done(((f32[3072,48]{1,0:T(8,128)}), f32[96,48]{1,0:T(8,128)}) %reduce-scatter.7.cloned.1.call-update) | async-done | bytes 18448
  128.3 0.9 copy.61
  129.3 2.5 psum.28
  131.8 30.7 %psum.29 = f32[48]{0:T(128)S(1)} all-reduce(f32[48]{0:T(128)S(1)} %psum.28), channel_id=1, replica_groups=mesh['dp'=16,'heads'=16,'side'=2] {'heads'}, use_global_device_ids=true, to_apply=%region_6.7 | all-reduce | flops 48 | bytes 384 | tf_op jit(solution)/shard_map/psum | solution.py:9
  162.6 1.0 scatter_custom_fusion
  163.8 14.2 %all_to_all.10 = bf16[16,2,432]{2,1,0:T(2,128)(2,1)S(1)} all-to-all(bf16[16,2,432]{2,1,0:T(2,128)(2,1)S(1)} %reshape.300), channel_id=1, replica_groups=mesh['dp'=16,'heads'=16,'side'=2] {'dp'}, dimensions={0} | all-to-all | bytes 55296 | tf_op jit(solution)/shard_map/all_to_all | solution.py:90
  178.2 0.4 copy.44
  178.5 75.2 %all_gather.3 = bf16[16,9,1536]{1,0,2:T(8,128)(2,1)} all-gather(bf16[16,9,96]{1,0,2:T(8,128)(2,1)S(1)} %copy.44), channel_id=1, replica_groups=mesh['dp'=16,'heads'=16,'side'=2] {'heads'}, dimensions={2}, use_global_device_ids=true | all-gather | bytes 470016 | tf_op jit(solution)/shard_map/all_gather | solution.py:97
  253.8 8.2 %reshape.288 = bf16[144,1536]{0,1:T(8,128)(2,1)S(1)} reshape(bf16[16,9,1536]{1,0,2:T(8,128)(2,1)} %all_gather.3) | data formatting | bytes 884736 | tf_op jit(solution)/shard_map/reshape | solution.py:98
  262.0 1.1 convolution_convert_fusion.1
  263.3 1.1 convolution_convert_fusion.2
  264.5 2.4 reshape_squeeze.11
  266.8 0.7 copy.46
  267.5 34.3 %all-reduce.7.cloned.1.call-done = (bf16[144,288]{1,0:T(8,128)(2,1)}, bf16[144,288]{1,0:T(8,128)(2,1)}) async-done(((bf16[144,288]{1,0:T(8,128)(2,1)}, bf16[144,288]{1,0:T(8,128)(2,1)}), (bf16[144,288]{1,0:T(8,128)(2,1)}, bf16[144,288]{1,0:T(8,128)(2,1)})) %all-reduce.7.cloned.1.call-update) | async-done | bytes 165904 | tf_op jit(solution)/shard_map/psum | solution.py:103
  301.8 1.0 fusion.23
  302.9 1.6 convolution_convert_fusion
  304.5 1.3 dynamic-slice
  305.9 1.7 fusion.4
  307.6 136.0 %all-reduce.5.cloned.1.call-done = bf16[16,9,16,96]{3,0,2,1:T(8,128)(2,1)} async-done(((bf16[16,9,16,96]{3,0,2,1:T(8,128)(2,1)}), bf16[16,9,16,96]{3,0,2,1:T(8,128)(2,1)}) %all-reduce.5.cloned.1.call-update) | async-done | bytes 442384
  443.6 1.4 constant_dynamic-slice_fusion
  445.0 0.7 reshape.302
  445.7 6.8 %all-to-all-start.1 = ((bf16[16,2,432]{2,1,0:T(2,128)(2,1)}), bf16[16,2,432]{2,1,0:T(2,128)(2,1)S(1)}, u32[]{:S(2)}, u32[]{:S(2)}) async-start(bf16[16,2,432]{2,1,0:T(2,128)(2,1)} %reshape.302), calls=%async_computation.1 | async-start | bytes 65536 | tf_op jit(solution)/shard_map/all_to_all | solution.py:112
  452.7 7.5 %all-to-all-done.1 = bf16[16,2,432]{2,1,0:T(2,128)(2,1)S(1)} async-done(((bf16[16,2,432]{2,1,0:T(2,128)(2,1)}), bf16[16,2,432]{2,1,0:T(2,128)(2,1)S(1)}, u32[]{:S(2)}, u32[]{:S(2)}) %all-to-all-start.1) | async-done | bytes 27680 | tf_op jit(solution)/shard_map/all_to_all | solution.py:112
  460.3 0.7 gather_fusion
  461.0 0.7 fusion.25
  (55 shorter events, 2.3 us)
Async XLA Ops:
  7.2 254.8 %copy-start = (bf16[1,16,96,288]{3,2,1,0:T(8,128)(2,1)S(1)}, bf16[1,16,96,288]{3,2,1,0:T(8,128)(2,1)}, u32[]{:S(2)}) copy-start(bf16[1,16,96,288]{3,2,1,0:T(8,128)(2,1)} %param.26) | copy-start | bytes 2654212
  7.2 5.3 %copy-start.2 = (bf16[24,1,128,128]{3,2,1,0:T(8,128)(2,1)S(1)}, bf16[24,1,128,128]{3,2,1,0:T(8,128)(2,1)}, u32[]{:S(2)}) copy-start(bf16[24,1,128,128]{3,2,1,0:T(8,128)(2,1)} %param.17) | copy-start | bytes 2359300
  7.2 121.1 %reduce-scatter.7.cloned.1.call-start = ((), (), s32[]{:S(2)}) async-start(), calls=%async_computation.3 | async-start | bytes 1622016
  12.5 2.0 copy-start.4
  12.5 2.1 copy-start.9
  14.5 1.7 copy-start.7
  16.2 113.0 %copy-start.6 = (bf16[24,2,96]{2,1,0:T(2,128)(2,1)S(1)}, bf16[24,2,96]{2,1,0:T(2,128)(2,1)}, u32[]{:S(2)}) copy-start(bf16[24,2,96]{2,1,0:T(2,128)(2,1)} %param.21) | copy-start | bytes 27652
  16.2 285.6 %all-reduce.7.cloned.1.call-start = ((), (), s32[]{:S(2)}) async-start(), calls=%async_computation.5 | async-start | bytes 442368 | tf_op jit(solution)/shard_map/psum | solution.py:103
  129.3 124.4 %copy-start.5 = (bf16[48,96]{1,0:T(8,128)(2,1)}, bf16[48,96]{1,0:T(8,128)(2,1)S(1)}, u32[]{:S(2)}) copy-start(bf16[48,96]{1,0:T(8,128)(2,1)S(1)} %get-tuple-element.6) | copy-start | bytes 27652
  262.0 1.3 copy-start.1
  264.4 179.2 %all-reduce.5.cloned.1.call-start = ((), (), s32[]{:S(2)}) async-start(), calls=%async_computation.4 | async-start | bytes 1179648
  267.5 38.3 %copy-start.3 = (bf16[24,1,128,128]{3,2,1,0:T(8,128)(2,1)S(1)}, bf16[24,1,128,128]{3,2,1,0:T(8,128)(2,1)}, u32[]{:S(2)}) copy-start(bf16[24,1,128,128]{3,2,1,0:T(8,128)(2,1)} %param.17) | copy-start | bytes 2359300
  304.5 148.0 %copy-start.8 = (f32[24,2,2]{0,2,1:T(2,128)S(1)}, f32[24,2,2]{0,2,1:T(2,128)}, u32[]{:S(2)}) copy-start(f32[24,2,2]{0,2,1:T(2,128)} %param.24) | copy-start | bytes 1156
  445.7 14.4 %all-to-all-start.1 = ((bf16[16,2,432]{2,1,0:T(2,128)(2,1)}), bf16[16,2,432]{2,1,0:T(2,128)(2,1)S(1)}, u32[]{:S(2)}, u32[]{:S(2)}) async-start(bf16[16,2,432]{2,1,0:T(2,128)(2,1)} %reshape.302), calls=%async_computation.1 | async-start | bytes 65536 | tf_op jit(solution)/shard_map/all_to_all | solution.py:112
Sparse Core Ops, SparseCore 0:
  16.3 111.9 reduce-scatter.6
  264.5 37.2 all-reduce.6
  304.6 138.8 all-reduce.4
